TPU v7x, 512 devices: a whole 4x4x16 slice. The times are simulated.
512 devices in a mesh: sub: 64 (over y, z), grp: 8 (over x, core).
Axes of the slice: x: 4, y: 4, z: 16, core: 2. Of those that a mesh axis runs over, the one named last changes fastest.
Arguments:
- margin_basis: bfloat16 [512, 6, 384, 128], P(('sub', 'grp')), may hold values from -6 to 6
- pair_matrix: bfloat16 [512, 6, 384, 384], P(('sub', 'grp')), as said below
- own_basis: bfloat16 [512, 2048, 128], P(('sub', 'grp')), may hold values from -0.125 to 0.125
- own_image: bfloat16 [512, 2048, 128], P(('sub', 'grp')), may hold values from -6 to 6
- tile_counts: int32 [512, 6], P(('sub', 'grp')), may hold values from 0 to 3, as said below
Outputs:
- coarse_rows: float32 [512, 7, 128, 128], P('sub', None, 'grp')
Inputs may be any that keep to these rules, and one draw needn't show every extreme that they name: `tile_counts`: tile counts of the two slots of one neighbour pair are equal, zero for slots without neighbour, and the pairs of subdomains 0 and 1 and of subdomains (31) * 8 and (32) * 8 have 3 tiles in every draw. pair_matrix[s + stride, 2j + 1] is the transpose of pair_matrix[s, 2j] wherever both are neighbours.
All inputs are finite; a program needn't handle non-finite values.
Results may differ from a plain program's by a relative error of at most 0.0026.
Values may be sent and summed in bfloat16 or wider, within the bound.
No kernel may reach another device: no remote copies, remote signals or barrier semaphores. Data moves between devices by JAX's collectives and lax.ppermute only.
A program may use at most 64 MiB of HBM per device.

v0:
```python
import jax
import jax.numpy as jnp
from jax import lax
from jax.sharding import PartitionSpec as P

ROW_TILE = 128
SPAN = 8


def shifted(value, axis, steps):
    count = lax.axis_size(axis)
    initial, last = (max(0, -steps), min(count, count - steps))
    return lax.ppermute(value, axis, [(source, source + steps) for source in range(initial, last)])


def masked(block, tile_count):
    row_index = lax.broadcasted_iota(jnp.int32, block.shape, 0)
    return jnp.where(row_index < tile_count * ROW_TILE, block, jnp.zeros((), block.dtype))


def contract_rows(left, right):
    return lax.dot_general(
        left, right, (((0,), (0,)), ((), ())), preferred_element_type=jnp.float32
    )


def apply_block(matrix, column_basis, flipped):
    if flipped:
        return contract_rows(matrix, column_basis)
    return jnp.dot(matrix, column_basis, preferred_element_type=jnp.float32)


def couple_pair(matrix, row_basis, column_basis, flipped):
    applied = apply_block(matrix, column_basis, flipped).astype(jnp.bfloat16)
    return contract_rows(row_basis, applied)


def local(margin_basis, pair_matrix, own_basis, own_image, tile_counts):
    own_margin = margin_basis[0]
    matrices = pair_matrix[0]
    counts = tile_counts[0]
    x_above = shifted(own_margin[1], "grp", -1)
    y_above = shifted(own_margin[3], "sub", -1)
    z_above = shifted(own_margin[5], "sub", -SPAN)
    diagonal_block = contract_rows(own_basis[0], own_image[0])
    received = (x_above, y_above, z_above)
    upper_blocks = []
    for which in range(3):
        upper = 2 * which
        upper_blocks.append(
            couple_pair(
                matrices[upper],
                masked(own_margin[upper], counts[upper]),
                masked(received[which], counts[upper]),
                False,
            )
        )
    x_below = shifted(own_margin[0], "grp", 1)
    y_below = shifted(own_margin[2], "sub", 1)
    z_below = shifted(own_margin[4], "sub", SPAN)
    from_below = (x_below, y_below, z_below)
    lower_blocks = []
    for which in range(3):
        lower = 2 * which + 1
        lower_blocks.append(
            couple_pair(
                matrices[lower],
                masked(from_below[which], counts[lower]),
                masked(own_margin[lower], counts[lower]),
                True,
            ).T
        )
    blocks = [diagonal_block]
    for which in range(3):
        blocks.append(upper_blocks[which])
        blocks.append(lower_blocks[which])
    coarse = jnp.stack(blocks, axis=0)[None]
    return lax.all_to_all(coarse, "grp", split_axis=2, concat_axis=0, tiled=True)


def solution(mesh):
    return jax.shard_map(
        local,
        mesh=mesh,
        in_specs=(
            P(("sub", "grp"), None, None, None),
            P(("sub", "grp"), None, None, None),
            P(("sub", "grp"), None, None),
            P(("sub", "grp"), None, None),
            P(("sub", "grp"), None),
        ),
        out_specs=P("sub", None, "grp", None),
        check_vma=False,
    )
```

profile of v0, /device:TPU:56, one launch (start us, length us, event | category | flops | bytes accessed | tf_op | source)
XLA Modules:
  0.0 73.5 jit_solution(1389235496003536955)
XLA Ops:
  0.0 0.0 copy-start
  0.0 0.0 copy-start.1
  0.0 1.3 %slice_bitcast_fusion = (bf16[384,128]{1,0:T(8,128)(2,1)S(1)}, bf16[384,128]{1,0:T(8,128)(2,1)S(1)}, bf16[384,128]{1,0:T(8,128)(2,1)S(1)}, bf16[384,128]{1,0:T(8...) fusion(bf16[1,6,384,128]{3,2,1,0:T(8,128)(2,1)} %param.5), kind=kLoop, calls=%fused_computation.47 | loop fusion | bytes 1179648 | tf_op jit(solution)/shard_map/squeeze | solution.py:53
  1.3 14.8 %collective-permute-start.5 = (bf16[384,128]{1,0:T(8,128)(2,1)S(1)}, bf16[384,128]{1,0:T(8,128)(2,1)S(1)}, u32[]{:S(2)}, u32[]{:S(2)}) collective-permute-start(bf16[384,128]{1,0:T(8,128)(2,1)S(1)} %get-tuple-element.5), channel_id=1, source_target_pairs={{0,64},{8,72},{16,80},{24,88},{32,96},{40,104},{48,112},{56,120},{... | collective-permute-start | bytes 294920 | tf_op jit(solution)/shard_map/ppermute | solution.py:13
  16.1 2.9 %collective-permute-start.2 = (bf16[384,128]{1,0:T(8,128)(2,1)S(1)}, bf16[384,128]{1,0:T(8,128)(2,1)S(1)}, u32[]{:S(2)}, u32[]{:S(2)}) collective-permute-start(bf16[384,128]{1,0:T(8,128)(2,1)S(1)} %get-tuple-element.6), channel_id=1, source_target_pairs={{8,0},{16,8},{24,16},{32,24},{40,32},{48,40},{56,48},{64,56},{72,6... | collective-permute-start | bytes 294920 | tf_op jit(solution)/shard_map/ppermute | solution.py:13
  19.0 2.9 %collective-permute-start.3 = (bf16[384,128]{1,0:T(8,128)(2,1)S(1)}, bf16[384,128]{1,0:T(8,128)(2,1)S(1)}, u32[]{:S(2)}, u32[]{:S(2)}) collective-permute-start(bf16[384,128]{1,0:T(8,128)(2,1)S(1)} %get-tuple-element.7), channel_id=1, source_target_pairs={{0,8},{8,16},{16,24},{24,32},{32,40},{40,48},{48,56},{56,64},{64,7... | collective-permute-start | bytes 294920 | tf_op jit(solution)/shard_map/ppermute | solution.py:13
  22.0 1.3 %collective-permute-start = (bf16[384,128]{1,0:T(8,128)(2,1)S(1)}, bf16[384,128]{1,0:T(8,128)(2,1)S(1)}, u32[]{:S(2)}, u32[]{:S(2)}) collective-permute-start(bf16[384,128]{1,0:T(8,128)(2,1)S(1)} %get-tuple-element.8), channel_id=1, source_target_pairs={{1,0},{2,1},{3,2},{4,3},{5,4},{6,5},{7,6},{9,8},{10,9},{11,10},{12... | collective-permute-start | bytes 294920 | tf_op jit(solution)/shard_map/ppermute | solution.py:13
  23.3 3.0 %collective-permute-start.1 = (bf16[384,128]{1,0:T(8,128)(2,1)S(1)}, bf16[384,128]{1,0:T(8,128)(2,1)S(1)}, u32[]{:S(2)}, u32[]{:S(2)}) collective-permute-start(bf16[384,128]{1,0:T(8,128)(2,1)S(1)} %get-tuple-element.9), channel_id=1, source_target_pairs={{0,1},{1,2},{2,3},{3,4},{4,5},{5,6},{6,7},{8,9},{9,10},{10,11},{11... | collective-permute-start | bytes 294920 | tf_op jit(solution)/shard_map/ppermute | solution.py:13
  26.3 1.5 %fusion.117 = (s32[1,1]{1,0:T(1,128)}, s32[1,1]{1,0:T(1,128)}, s32[1,1]{1,0:T(1,128)}, s32[1,1]{1,0:T(1,128)}, s32[1,1]{1,0:T(1,128)}, /*index=5*/s32[1,1]{1,0:T(1,128)}) fusion(s32[1,6]{1,0:T(1,128)} %param.9), kind=kLoop, calls=%fused_computation.94 | loop fusion | bytes 48 | tf_op jit(solution)/shard_map/slice | solution.py:68
  31.6 0.0 copy-done
  31.6 1.4 %fusion.6 = f32[7,128,128]{2,1,0:T(8,128)S(1)} fusion(bf16[1,2048,128]{2,1,0:T(8,128)(2,1)S(1)} %copy-done, bf16[1,2048,128]{2,1,0:T(8,128)(2,1)} %param.7), kind=kOutput, calls=%fused_computation.13 | convolution fusion | flops 67108864 | bytes 1114112 | tf_op jit(solution)/shard_map/dot_general | solution.py:22
  33.0 0.0 collective-permute-done
  33.1 2.1 %collective-permute-start.4 = (bf16[384,128]{1,0:T(8,128)(2,1)S(1)}, bf16[384,128]{1,0:T(8,128)(2,1)S(1)}, u32[]{:S(2)}, u32[]{:S(2)}) collective-permute-start(bf16[384,128]{1,0:T(8,128)(2,1)S(1)} %get-tuple-element.10), channel_id=1, source_target_pairs={{64,0},{72,8},{80,16},{88,24},{96,32},{104,40},{112,48},{120,56},{... | collective-permute-start | bytes 294920 | tf_op jit(solution)/shard_map/ppermute | solution.py:13
  35.2 0.0 copy-done.1
  35.2 1.5 %fusion.18 = f32[7,128,128]{2,1,0:T(8,128)S(1)} fusion(f32[7,128,128]{2,1,0:T(8,128)S(1)} %fusion.6, bf16[1,6,384,384]{3,2,1,0:T(8,128)(2,1)} %param.6, bf16[384,128]{1,0:T(8,128)(2,1)S(1)} %collective-permute-done, pred[384]{0:T(512)(128)(4,1)S(1)} %iota_compare_fusion.5, bf16[1,6,384,128]{3,2,1,0:T(8,128)(2,1)S(1)} %copy-done.1), kind=kOutput, calls=%fused_computation.25 | convolution fusion | flops 50479104 | bytes 558080 | tf_op jit(solution)/shard_map/dot_general | solution.py:22
  36.6 0.0 collective-permute-done.1
  36.7 1.4 %fusion.16 = f32[7,128,128]{2,1,0:T(8,128)S(1)} fusion(f32[7,128,128]{2,1,0:T(8,128)S(1)} %fusion.18, bf16[1,6,384,384]{3,2,1,0:T(8,128)(2,1)} %param.6, bf16[384,128]{1,0:T(8,128)(2,1)S(1)} %collective-permute-done.1, pred[384]{0:T(512)(128)(4,1)S(1)} %iota_compare_fusion.4, bf16[1,6,384,128]{3,2,1,0:T(8,128)(2,1)S(1)} %copy-done.1), kind=kOutput, calls=%fused_computation.23 | convolution fusion | flops 50479104 | bytes 558080 | tf_op jit(solution)/shard_map/dot_general | solution.py:22
  38.1 0.0 collective-permute-done.2
  38.1 1.5 %fusion.14 = f32[7,128,128]{2,1,0:T(8,128)S(1)} fusion(f32[7,128,128]{2,1,0:T(8,128)S(1)} %fusion.16, bf16[1,6,384,384]{3,2,1,0:T(8,128)(2,1)} %param.6, bf16[384,128]{1,0:T(8,128)(2,1)S(1)} %collective-permute-done.2, pred[384]{0:T(512)(128)(4,1)S(1)} %iota_compare_fusion.3, bf16[1,6,384,128]{3,2,1,0:T(8,128)(2,1)S(1)} %copy-done.1), kind=kOutput, calls=%fused_computation.21 | convolution fusion | flops 50479104 | bytes 558080 | tf_op jit(solution)/shard_map/dot_general | solution.py:22
  39.6 0.0 collective-permute-done.3
  39.6 1.4 %fusion.12 = f32[7,128,128]{2,1,0:T(8,128)S(1)} fusion(f32[7,128,128]{2,1,0:T(8,128)S(1)} %fusion.14, bf16[1,6,384,384]{3,2,1,0:T(8,128)(2,1)} %param.6, bf16[384,128]{1,0:T(8,128)(2,1)S(1)} %collective-permute-done.3, pred[384]{0:T(512)(128)(4,1)S(1)} %iota_compare_fusion.2, bf16[1,6,384,128]{3,2,1,0:T(8,128)(2,1)S(1)} %copy-done.1), kind=kOutput, calls=%fused_computation.19 | convolution fusion | flops 50479104 | bytes 558080 | tf_op jit(solution)/shard_map/dot_general | solution.py:22
  41.0 13.2 %collective-permute-done.4 = bf16[384,128]{1,0:T(8,128)(2,1)S(1)} collective-permute-done((bf16[384,128]{1,0:T(8,128)(2,1)S(1)}, bf16[384,128]{1,0:T(8,128)(2,1)S(1)}, u32[]{:S(2)}, u32[]{:S(2)}) %collective-permute-start.4) | collective-permute-done | bytes 98336 | tf_op jit(solution)/shard_map/ppermute | solution.py:13
  54.3 1.5 %fusion.10 = f32[7,128,128]{2,1,0:T(8,128)S(1)} fusion(f32[7,128,128]{2,1,0:T(8,128)S(1)} %fusion.12, bf16[1,6,384,384]{3,2,1,0:T(8,128)(2,1)} %param.6, bf16[384,128]{1,0:T(8,128)(2,1)S(1)} %collective-permute-done.4, pred[384]{0:T(512)(128)(4,1)S(1)} %iota_compare_fusion.1, bf16[1,6,384,128]{3,2,1,0:T(8,128)(2,1)S(1)} %copy-done.1), kind=kOutput, calls=%fused_computation.17 | convolution fusion | flops 50479104 | bytes 558080 | tf_op jit(solution)/shard_map/dot_general | solution.py:22
  55.7 0.0 collective-permute-done.5
  55.7 1.4 %fusion.8 = f32[7,128,128]{2,1,0:T(8,128)S(1)} fusion(f32[7,128,128]{2,1,0:T(8,128)S(1)} %fusion.10, bf16[1,6,384,384]{3,2,1,0:T(8,128)(2,1)} %param.6, bf16[384,128]{1,0:T(8,128)(2,1)S(1)} %collective-permute-done.5, pred[384]{0:T(512)(128)(4,1)S(1)} %iota_compare_fusion, bf16[1,6,384,128]{3,2,1,0:T(8,128)(2,1)S(1)} %copy-done.1), kind=kOutput, calls=%fused_computation.15 | convolution fusion | flops 50479104 | bytes 558080 | tf_op jit(solution)/shard_map/dot_general | solution.py:22
  57.2 0.5 copy.11
  57.6 15.0 %all_to_all.18 = f32[1,7,128,128]{3,0,1,2:T(1,128)S(1)} all-to-all(f32[1,7,128,128]{3,0,1,2:T(1,128)S(1)} %copy.11), channel_id=1, replica_groups=mesh['sub'=64,'grp'=8] {'grp'}, dimensions={2} | all-to-all | bytes 917504 | tf_op jit(solution)/shard_map/all_to_all | solution.py:78
  72.7 0.8 %copy.13 = f32[8,7,16,128]{3,2,1,0:T(8,128)} copy(f32[8,7,16,128]{3,2,0,1:T(8,128)S(1)} %bitcast.103) | data formatting | bytes 917504 | tf_op jit(solution)/shard_map/all_to_all | solution.py:78
  (7 shorter events, 0.1 us)
Async XLA Ops:
  0.0 31.6 %copy-start = (bf16[1,2048,128]{2,1,0:T(8,128)(2,1)S(1)}, bf16[1,2048,128]{2,1,0:T(8,128)(2,1)}, u32[]{:S(2)}) copy-start(bf16[1,2048,128]{2,1,0:T(8,128)(2,1)} %param.8) | copy-start | bytes 1572868
  0.0 35.2 %copy-start.1 = (bf16[1,6,384,128]{3,2,1,0:T(8,128)(2,1)S(1)}, bf16[1,6,384,128]{3,2,1,0:T(8,128)(2,1)}, u32[]{:S(2)}) copy-start(bf16[1,6,384,128]{3,2,1,0:T(8,128)(2,1)} %param.5) | copy-start | bytes 1769476
  1.3 54.4 %collective-permute-start.5 = (bf16[384,128]{1,0:T(8,128)(2,1)S(1)}, bf16[384,128]{1,0:T(8,128)(2,1)S(1)}, u32[]{:S(2)}, u32[]{:S(2)}) collective-permute-start(bf16[384,128]{1,0:T(8,128)(2,1)S(1)} %get-tuple-element.5), channel_id=1, source_target_pairs={{0,64},{8,72},{16,80},{24,88},{32,96},{40,104},{48,112},{56,120},{... | collective-permute-start | bytes 294920 | tf_op jit(solution)/shard_map/ppermute | solution.py:13
  16.1 22.0 %collective-permute-start.2 = (bf16[384,128]{1,0:T(8,128)(2,1)S(1)}, bf16[384,128]{1,0:T(8,128)(2,1)S(1)}, u32[]{:S(2)}, u32[]{:S(2)}) collective-permute-start(bf16[384,128]{1,0:T(8,128)(2,1)S(1)} %get-tuple-element.6), channel_id=1, source_target_pairs={{8,0},{16,8},{24,16},{32,24},{40,32},{48,40},{56,48},{64,56},{72,6... | collective-permute-start | bytes 294920 | tf_op jit(solution)/shard_map/ppermute | solution.py:13
  19.0 20.6 %collective-permute-start.3 = (bf16[384,128]{1,0:T(8,128)(2,1)S(1)}, bf16[384,128]{1,0:T(8,128)(2,1)S(1)}, u32[]{:S(2)}, u32[]{:S(2)}) collective-permute-start(bf16[384,128]{1,0:T(8,128)(2,1)S(1)} %get-tuple-element.7), channel_id=1, source_target_pairs={{0,8},{8,16},{16,24},{24,32},{32,40},{40,48},{48,56},{56,64},{64,7... | collective-permute-start | bytes 294920 | tf_op jit(solution)/shard_map/ppermute | solution.py:13
  22.0 11.1 %collective-permute-start = (bf16[384,128]{1,0:T(8,128)(2,1)S(1)}, bf16[384,128]{1,0:T(8,128)(2,1)S(1)}, u32[]{:S(2)}, u32[]{:S(2)}) collective-permute-start(bf16[384,128]{1,0:T(8,128)(2,1)S(1)} %get-tuple-element.8), channel_id=1, source_target_pairs={{1,0},{2,1},{3,2},{4,3},{5,4},{6,5},{7,6},{9,8},{10,9},{11,10},{12... | collective-permute-start | bytes 294920 | tf_op jit(solution)/shard_map/ppermute | solution.py:13
  23.3 13.4 %collective-permute-start.1 = (bf16[384,128]{1,0:T(8,128)(2,1)S(1)}, bf16[384,128]{1,0:T(8,128)(2,1)S(1)}, u32[]{:S(2)}, u32[]{:S(2)}) collective-permute-start(bf16[384,128]{1,0:T(8,128)(2,1)S(1)} %get-tuple-element.9), channel_id=1, source_target_pairs={{0,1},{1,2},{2,3},{3,4},{4,5},{5,6},{6,7},{8,9},{9,10},{10,11},{11... | collective-permute-start | bytes 294920 | tf_op jit(solution)/shard_map/ppermute | solution.py:13
  33.1 21.2 %collective-permute-start.4 = (bf16[384,128]{1,0:T(8,128)(2,1)S(1)}, bf16[384,128]{1,0:T(8,128)(2,1)S(1)}, u32[]{:S(2)}, u32[]{:S(2)}) collective-permute-start(bf16[384,128]{1,0:T(8,128)(2,1)S(1)} %get-tuple-element.10), channel_id=1, source_target_pairs={{64,0},{72,8},{80,16},{88,24},{96,32},{104,40},{112,48},{120,56},{... | collective-permute-start | bytes 294920 | tf_op jit(solution)/shard_map/ppermute | solution.py:13
where the time goes:
time: 74.1 us; the launch traced here: 73.5 us
  starting transfers between devices  27.1 us (37%)
  blocking collectives  15 us (20%)
  waiting for transfers between devices  13.2 us (18%)
  matrix products  10.1 us (14%)
  local copies, waits for them, and re-layouts  4.1 us (6%)
  between operations  3.94 us (5%)
    ppermute x6, starting transfers between devices, shifted(): lax.ppermute(value, axis, [(source, source + steps) for source in range(i...  27.1 us
    all_to_all x1, blocking collectives, local(): lax.all_to_all(coarse, 'grp', split_axis=2, concat_axis=0, tiled=True)  15 us
    ppermute x6, waiting for transfers between devices, shifted(): lax.ppermute(value, axis, [(source, source + steps) for source in range(i...  13.2 us
    dot_general x7, matrix products, contract_rows(): lax.dot_general(left, right, (((0,), (0,)), ((), ())), preferred_element_...  10.1 us
    slice x1, local copies, waits for them, and re-layouts, local(): counts[lower]  1.53 us
  transfers between devices with their start and end apart: 6, of which 1 were waited for; matrix products, arithmetic and copies ran while one was open for 14% of the time, Pallas kernels for 0%

commit v1 on v0

v1 whole, which is shorter than its diff:
```python
import jax
import jax.numpy as jnp
from jax import lax
from jax.experimental import pallas as pl
from jax.experimental.pallas import tpu as pltpu
from jax.sharding import PartitionSpec as P


ROW_TILE = 128
SPAN = 8
EIG = 128
ROWS = 384
SHARE = 16


def shifted(value, axis, steps):
    count = lax.axis_size(axis)
    initial, last = (max(0, -steps), min(count, count - steps))
    return lax.ppermute(value, axis, [(source, source + steps) for source in range(initial, last)])


def masked(block, tile_count):
    row_index = lax.broadcasted_iota(jnp.int32, block.shape, 0)
    return jnp.where(row_index < tile_count * ROW_TILE, block, jnp.zeros((), block.dtype))


def contract_rows(left, right):
    return lax.dot_general(
        left, right, (((0,), (0,)), ((), ())), preferred_element_type=jnp.float32
    )


def upper_block(basis, matrix, received, count):
    image = jnp.dot(matrix, masked(received, count), preferred_element_type=jnp.float32)
    return contract_rows(masked(basis, count), image.astype(jnp.bfloat16))


def lower_left(basis, matrix, count):
    return contract_rows(masked(basis, count), matrix).astype(jnp.bfloat16)


def lower_block(left, received, count):
    return jnp.dot(left, masked(received, count), preferred_element_type=jnp.float32)


def shares(block):
    return block.astype(jnp.bfloat16).reshape(EIG // SHARE, SHARE, EIG)


def near_kernel(counts, margin, matrices, own_basis, own_image, x_above, y_above, y_below, out, z_left):
    z_left[...] = lower_left(margin[0, 5], matrices[0, 5], counts[0, 5])
    out[:, 0] = shares(contract_rows(own_basis[0], own_image[0]))
    along_x = upper_block(margin[0, 0], matrices[0, 0], x_above[...], counts[0, 0])
    out[:, 1] = shares(along_x)
    out[:, 2] = shares(along_x.T)
    out[:, 3] = shares(upper_block(margin[0, 2], matrices[0, 2], y_above[...], counts[0, 2]))
    left = lower_left(margin[0, 3], matrices[0, 3], counts[0, 3])
    out[:, 4] = shares(lower_block(left, y_below[...], counts[0, 3]))


def far_kernel(counts, margin, matrix, left, z_above, z_below, near, out):
    out[:, :5] = near[...]
    out[:, 5] = shares(upper_block(margin[0, 0], matrix[0, 0], z_above[...], counts[0, 4]))
    out[:, 6] = shares(lower_block(left[...], z_below[...], counts[0, 5]))


def spread_kernel(rows, out):
    out[:, :2] = rows[:, :2].astype(jnp.float32)
    out[0, 2] = jnp.zeros((SHARE, EIG), jnp.float32)
    out[1:, 2] = rows[:-1, 2].astype(jnp.float32)
    out[:, 3:] = rows[:, 3:].astype(jnp.float32)


def on_chip(value):
    return pltpu.with_memory_space_constraint(value, pltpu.VMEM)


def local(margin_basis, pair_matrix, own_basis, own_image, tile_counts):
    smem = pl.BlockSpec(memory_space=pltpu.SMEM)
    vmem = pl.BlockSpec(memory_space=pltpu.VMEM)
    far_up, far_down = margin_basis[0, 5], margin_basis[0, 4]
    far_up, far_down, margin = lax.optimization_barrier((far_up, far_down, margin_basis))
    z_above = shifted(far_up, "sub", -SPAN)
    z_below = shifted(far_down, "sub", SPAN)
    x_above = shifted(margin[0, 1], "grp", -1)
    y_above = shifted(margin[0, 3], "sub", -1)
    y_below = shifted(margin[0, 2], "sub", 1)
    near, z_left = pl.pallas_call(
        near_kernel,
        out_shape=(
            pltpu.VMEM((8, 5, SHARE, EIG), jnp.bfloat16),
            pltpu.VMEM((EIG, ROWS), jnp.bfloat16),
        ),
        in_specs=[smem] + [vmem] * 7,
        out_specs=(vmem, vmem),
    )(
        tile_counts,
        margin_basis,
        pair_matrix,
        own_basis,
        own_image,
        on_chip(x_above),
        on_chip(y_above),
        on_chip(y_below),
    )
    coarse = pl.pallas_call(
        far_kernel,
        grid=(1,),
        out_shape=pltpu.VMEM((8, 7, SHARE, EIG), jnp.bfloat16),
        in_specs=[
            smem,
            pl.BlockSpec((1, 1, ROWS, EIG), lambda i: (0, 4, 0, 0)),
            pl.BlockSpec((1, 1, ROWS, ROWS), lambda i: (0, 4, 0, 0)),
            vmem,
            vmem,
            vmem,
            vmem,
        ],
        out_specs=vmem,
    )(
        tile_counts,
        margin_basis,
        pair_matrix,
        on_chip(z_left),
        on_chip(z_above),
        on_chip(z_below),
        on_chip(near),
    )
    rows = lax.all_to_all(coarse, "grp", split_axis=0, concat_axis=0, tiled=True)
    return pl.pallas_call(
        spread_kernel,
        out_shape=jax.ShapeDtypeStruct((8, 7, SHARE, EIG), jnp.float32),
        in_specs=[vmem],
        out_specs=vmem,
    )(on_chip(rows))


def solution(mesh):
    return jax.shard_map(
        local,
        mesh=mesh,
        in_specs=(
            P(("sub", "grp"), None, None, None),
            P(("sub", "grp"), None, None, None),
            P(("sub", "grp"), None, None),
            P(("sub", "grp"), None, None),
            P(("sub", "grp"), None),
        ),
        out_specs=P("sub", None, "grp", None),
        check_vma=False,
    )
```

time: 74.1 us -> 61.6 us (0.83)
  matrix products: 10.1 us -> 0 us
  waiting for transfers between devices: 13.2 us -> 18.7 us
  Pallas kernels: 0 us -> 5.23 us
  between operations: 3.94 us -> 0.08 us
  blocking collectives: 15 us -> 11.2 us
  starting transfers between devices: 27.1 us -> 24.1 us
  local copies, waits for them, and re-layouts: 4.1 us -> 1.97 us
    dot_general x7 -> x0, matrix products: 10.1 us -> none  [contract_rows(): lax.dot_general(left, right, (((0,), (0,)), ((), ())), preferred_element_...]
    ppermute x6 -> x5, waiting for transfers between devices: 13.2 us -> 18.7 us  [shifted(): lax.ppermute(value, axis, [(source, source + steps) for source in range(i...]
    pallas_call x0 -> x3, Pallas kernels: none -> 5.23 us  [the longest x1 2.96 us: local(): pl.pallas_call(near_kernel, out_shape=(pltpu.VMEM((8, 5, SHARE, EIG), jnp...]
    all_to_all x1, blocking collectives: 15 us -> 11.2 us  [local(): lax.all_to_all(coarse, 'grp', split_axis=0, concat_axis=0, tiled=True)]
    ppermute x6 -> x5, starting transfers between devices: 27.1 us -> 24.1 us  [shifted(): lax.ppermute(value, axis, [(source, source + steps) for source in range(i...]
    slice x1 -> x0, local copies, waits for them, and re-layouts: 1.53 us -> none  [local(): counts[lower]]
    all_to_all x2 -> x0, local copies, waits for them, and re-layouts: 0.83 us -> none  [local(): lax.all_to_all(coarse, 'grp', split_axis=2, concat_axis=0, tiled=True)]
    squeeze x1 -> x2, local copies, waits for them, and re-layouts: 1.26 us -> 1.97 us  [the longest x1 1.01 us: local(): y_below = shifted(margin[0, 2], 'sub', 1)]
  transfers between devices with their start and end apart: 6 -> 5, of which waited for: 1 -> 2; matrix products, arithmetic and copies ran while one was open for 14% -> 0% of each run, Pallas kernels for 0% -> 5%
where the time goes in v1:
time: 61.6 us; the launch traced here: 61.2 us
  starting transfers between devices  24.1 us (39%)
  waiting for transfers between devices  18.7 us (30%)
  blocking collectives  11.2 us (18%)
  Pallas kernels  5.23 us (8%)
  local copies, waits for them, and re-layouts  1.97 us (3%)
    ppermute x5, starting transfers between devices, shifted(): lax.ppermute(value, axis, [(source, source + steps) for source in range(i...  24.1 us
    ppermute x5, waiting for transfers between devices, shifted(): lax.ppermute(value, axis, [(source, source + steps) for source in range(i...  18.7 us
    all_to_all x1, blocking collectives, local(): lax.all_to_all(coarse, 'grp', split_axis=0, concat_axis=0, tiled=True)  11.2 us
    pallas_call x1, Pallas kernels, local(): pl.pallas_call(near_kernel, out_shape=(pltpu.VMEM((8, 5, SHARE, EIG), jnp...  2.96 us
    pallas_call x1, Pallas kernels, local(): pl.pallas_call(far_kernel, grid=(1,), out_shape=pltpu.VMEM((8, 7, SHARE,...  1.47 us
  transfers between devices with their start and end apart: 5, of which 2 were waited for; matrix products, arithmetic and copies ran while one was open for 0% of the time, Pallas kernels for 5%

profile of v1, /device:TPU:56, one launch (start us, length us, event | category | flops | bytes accessed | tf_op | source)
XLA Modules:
  0.0 61.2 jit_solution(1562236191959487070)
XLA Ops:
  0.0 1.0 %slice_bitcast_fusion.3 = (bf16[384,128]{1,0:T(8,128)(2,1)S(1)}, bf16[384,128]{1,0:T(8,128)(2,1)S(1)}) fusion(bf16[1,6,384,128]{3,2,1,0:T(8,128)(2,1)} %margin.3), kind=kLoop, calls=%fused_computation.3 | loop fusion | bytes 393216 | tf_op jit(solution)/shard_map/squeeze | solution.py:81
  1.0 1.0 %slice_bitcast_fusion = (bf16[384,128]{1,0:T(8,128)(2,1)S(1)}, bf16[384,128]{1,0:T(8,128)(2,1)S(1)}, bf16[384,128]{1,0:T(8,128)(2,1)S(1)}) fusion(bf16[1,6,384,128]{3,2,1,0:T(8,128)(2,1)} %margin.3), kind=kLoop, calls=%fused_computation | loop fusion | bytes 589824 | tf_op jit(solution)/shard_map/squeeze | solution.py:87
  2.0 3.8 %collective-permute-start.2 = (bf16[384,128]{1,0:T(8,128)(2,1)S(1)}, bf16[384,128]{1,0:T(8,128)(2,1)S(1)}, u32[]{:S(2)}, u32[]{:S(2)}) collective-permute-start(bf16[384,128]{1,0:T(8,128)(2,1)S(1)} %get-tuple-element.15), channel_id=1, source_target_pairs={{0,8},{8,16},{16,24},{24,32},{32,40},{40,48},{48,56},{56,64},{64,7... | collective-permute-start | bytes 294920 | tf_op jit(solution)/shard_map/ppermute | solution.py:19
  5.8 2.0 %collective-permute-start.1 = (bf16[384,128]{1,0:T(8,128)(2,1)S(1)}, bf16[384,128]{1,0:T(8,128)(2,1)S(1)}, u32[]{:S(2)}, u32[]{:S(2)}) collective-permute-start(bf16[384,128]{1,0:T(8,128)(2,1)S(1)} %get-tuple-element.16), channel_id=1, source_target_pairs={{8,0},{16,8},{24,16},{32,24},{40,32},{48,40},{56,48},{64,56},{72,6... | collective-permute-start | bytes 294920 | tf_op jit(solution)/shard_map/ppermute | solution.py:19
  7.8 1.3 %collective-permute-start = (bf16[384,128]{1,0:T(8,128)(2,1)S(1)}, bf16[384,128]{1,0:T(8,128)(2,1)S(1)}, u32[]{:S(2)}, u32[]{:S(2)}) collective-permute-start(bf16[384,128]{1,0:T(8,128)(2,1)S(1)} %get-tuple-element.17), channel_id=1, source_target_pairs={{1,0},{2,1},{3,2},{4,3},{5,4},{6,5},{7,6},{9,8},{10,9},{11,10},{12... | collective-permute-start | bytes 294920 | tf_op jit(solution)/shard_map/ppermute | solution.py:19
  9.1 15.0 %collective-permute-start.3 = (bf16[384,128]{1,0:T(8,128)(2,1)S(1)}, bf16[384,128]{1,0:T(8,128)(2,1)S(1)}, u32[]{:S(2)}, u32[]{:S(2)}) collective-permute-start(bf16[384,128]{1,0:T(8,128)(2,1)S(1)} %get-tuple-element.12), channel_id=1, source_target_pairs={{64,0},{72,8},{80,16},{88,24},{96,32},{104,40},{112,48},{120,56},{... | collective-permute-start | bytes 294920 | tf_op jit(solution)/shard_map/ppermute | solution.py:19
  24.1 1.9 %collective-permute-start.4 = (bf16[384,128]{1,0:T(8,128)(2,1)S(1)}, bf16[384,128]{1,0:T(8,128)(2,1)S(1)}, u32[]{:S(2)}, u32[]{:S(2)}) collective-permute-start(bf16[384,128]{1,0:T(8,128)(2,1)S(1)} %get-tuple-element.13), channel_id=1, source_target_pairs={{0,64},{8,72},{16,80},{24,88},{32,96},{40,104},{48,112},{56,120},{... | collective-permute-start | bytes 294920 | tf_op jit(solution)/shard_map/ppermute | solution.py:19
  26.1 0.0 collective-permute-done.2.y_below
  26.1 0.0 collective-permute-done.1.y_above
  26.1 0.0 collective-permute-done.x_above
  26.1 3.0 %shard_map.55 = (bf16[8,5,16,128]{3,2,1,0:T(8,128)(2,1)S(1)}, bf16[128,384]{1,0:T(8,128)(2,1)S(1)}) custom-call(s32[1,6]{1,0:T(1,128)} %counts.3, bf16[1,6,384,128]{3,2,1,0:T(8,128)(2,1)} %margin.3, bf16[1,6,384,384]{3,2,1,0:T(8,128)(2,1)} %matrix.1, bf16[1,2048,128]{2,1,0:T(8,128)(2,1)} %own_basis.1, bf16[1,2048,128]{2,1,0:T(8,128)(2,1)} %own_image.1, ...), custom_call_target="tpu_custom_call" | custom-call | tf_op jit(solution)/shard_map/pallas_call | solution.py:88
  29.1 10.7 %collective-permute-done.3.z_above = bf16[384,128]{1,0:T(8,128)(2,1)S(1)} collective-permute-done((bf16[384,128]{1,0:T(8,128)(2,1)S(1)}, bf16[384,128]{1,0:T(8,128)(2,1)S(1)}, u32[]{:S(2)}, u32[]{:S(2)}) %collective-permute-start.3) | collective-permute-done | bytes 98336 | tf_op jit(solution)/shard_map/ppermute | solution.py:19
  39.8 7.9 %collective-permute-done.4.z_below = bf16[384,128]{1,0:T(8,128)(2,1)S(1)} collective-permute-done((bf16[384,128]{1,0:T(8,128)(2,1)S(1)}, bf16[384,128]{1,0:T(8,128)(2,1)S(1)}, u32[]{:S(2)}, u32[]{:S(2)}) %collective-permute-start.4) | collective-permute-done | bytes 98336 | tf_op jit(solution)/shard_map/ppermute | solution.py:19
  47.7 1.5 %shard_map.56 = bf16[8,7,16,128]{3,2,1,0:T(8,128)(2,1)S(1)} custom-call(s32[1,6]{1,0:T(1,128)} %counts.3, bf16[1,6,384,128]{3,2,1,0:T(8,128)(2,1)} %margin.3, bf16[1,6,384,384]{3,2,1,0:T(8,128)(2,1)} %matrix.1, bf16[128,384]{1,0:T(8,128)(2,1)S(1)} %get-tuple-element.11.left, bf16[384,128]{1,0:T(8,128)(2,1)S(1)} %collective-permute-done.3.z_above, ...), custom_call_target="tpu_custom_call" | custom-call | tf_op jit(solution)/shard_map/pallas_call | solution.py:106
  49.2 11.2 %all_to_all.5.rows = bf16[8,7,16,128]{3,2,1,0:T(8,128)(2,1)S(1)} all-to-all(bf16[8,7,16,128]{3,2,1,0:T(8,128)(2,1)S(1)} %shard_map.56), channel_id=1, replica_groups=mesh['sub'=64,'grp'=8] {'grp'}, dimensions={0} | all-to-all | bytes 458752 | tf_op jit(solution)/shard_map/all_to_all | solution.py:129
  60.5 0.8 %shard_map.57 = f32[8,7,16,128]{3,2,1,0:T(8,128)} custom-call(bf16[8,7,16,128]{3,2,1,0:T(8,128)(2,1)S(1)} %all_to_all.5.rows), custom_call_target="tpu_custom_call" | custom-call | tf_op jit(solution)/shard_map/pallas_call | solution.py:130
Async XLA Ops:
  2.0 24.1 %collective-permute-start.2 = (bf16[384,128]{1,0:T(8,128)(2,1)S(1)}, bf16[384,128]{1,0:T(8,128)(2,1)S(1)}, u32[]{:S(2)}, u32[]{:S(2)}) collective-permute-start(bf16[384,128]{1,0:T(8,128)(2,1)S(1)} %get-tuple-element.15), channel_id=1, source_target_pairs={{0,8},{8,16},{16,24},{24,32},{32,40},{40,48},{48,56},{56,64},{64,7... | collective-permute-start | bytes 294920 | tf_op jit(solution)/shard_map/ppermute | solution.py:19
  5.8 20.3 %collective-permute-start.1 = (bf16[384,128]{1,0:T(8,128)(2,1)S(1)}, bf16[384,128]{1,0:T(8,128)(2,1)S(1)}, u32[]{:S(2)}, u32[]{:S(2)}) collective-permute-start(bf16[384,128]{1,0:T(8,128)(2,1)S(1)} %get-tuple-element.16), channel_id=1, source_target_pairs={{8,0},{16,8},{24,16},{32,24},{40,32},{48,40},{56,48},{64,56},{72,6... | collective-permute-start | bytes 294920 | tf_op jit(solution)/shard_map/ppermute | solution.py:19
  7.8 18.3 %collective-permute-start = (bf16[384,128]{1,0:T(8,128)(2,1)S(1)}, bf16[384,128]{1,0:T(8,128)(2,1)S(1)}, u32[]{:S(2)}, u32[]{:S(2)}) collective-permute-start(bf16[384,128]{1,0:T(8,128)(2,1)S(1)} %get-tuple-element.17), channel_id=1, source_target_pairs={{1,0},{2,1},{3,2},{4,3},{5,4},{6,5},{7,6},{9,8},{10,9},{11,10},{12... | collective-permute-start | bytes 294920 | tf_op jit(solution)/shard_map/ppermute | solution.py:19
  9.1 30.7 %collective-permute-start.3 = (bf16[384,128]{1,0:T(8,128)(2,1)S(1)}, bf16[384,128]{1,0:T(8,128)(2,1)S(1)}, u32[]{:S(2)}, u32[]{:S(2)}) collective-permute-start(bf16[384,128]{1,0:T(8,128)(2,1)S(1)} %get-tuple-element.12), channel_id=1, source_target_pairs={{64,0},{72,8},{80,16},{88,24},{96,32},{104,40},{112,48},{120,56},{... | collective-permute-start | bytes 294920 | tf_op jit(solution)/shard_map/ppermute | solution.py:19
  24.1 23.6 %collective-permute-start.4 = (bf16[384,128]{1,0:T(8,128)(2,1)S(1)}, bf16[384,128]{1,0:T(8,128)(2,1)S(1)}, u32[]{:S(2)}, u32[]{:S(2)}) collective-permute-start(bf16[384,128]{1,0:T(8,128)(2,1)S(1)} %get-tuple-element.13), channel_id=1, source_target_pairs={{0,64},{8,72},{16,80},{24,88},{32,96},{40,104},{48,112},{56,120},{... | collective-permute-start | bytes 294920 | tf_op jit(solution)/shard_map/ppermute | solution.py:19

commit v2 on v1

v2 whole, which is shorter than its diff:
```python
import jax
import jax.numpy as jnp
from jax import lax
from jax.experimental import pallas as pl
from jax.experimental.pallas import tpu as pltpu
from jax.sharding import PartitionSpec as P


ROW_TILE = 128
SPAN = 8
EIG = 128
ROWS = 384
SHARE = 16


def moved(value, axis, steps, sends):
    count = lax.axis_size(axis)
    pairs = [(i, i + steps) for i in range(count) if sends(i) and 0 <= i + steps < count]
    return lax.ppermute(value, axis, pairs)


def anyone(line):
    return True


EXCHANGES = {
    "z_up": (5, 4, "sub", -SPAN, anyone),
    "z_down": (4, 5, "sub", SPAN, anyone),
    "x_up": (1, 0, "grp", -1, anyone),
    "y_up": (3, 2, "sub", -1, anyone),
    "y_down": (2, 3, "sub", 1, anyone),
}
ORDER = tuple(EXCHANGES)


def masked(block, tile_count, dim=0):
    index = lax.broadcasted_iota(jnp.int32, block.shape, dim)
    return jnp.where(index < tile_count * ROW_TILE, block, jnp.zeros((), block.dtype))


def contract_rows(left, right):
    return lax.dot_general(
        left, right, (((0,), (0,)), ((), ())), preferred_element_type=jnp.float32
    )


def times(left, right):
    return jnp.dot(left, right, preferred_element_type=jnp.float32)


def shares(block):
    return block.astype(jnp.bfloat16).reshape(EIG // SHARE, SHARE, EIG)


def total(blocks):
    value = blocks[0][...]
    for block in blocks[1:]:
        value = value + block[...]
    return value


def near_kernel(counts, margin, matrices, own_basis, own_image, x_above, out, left):
    for k in range(2, 6):
        product = masked(
            contract_rows(masked(margin[0, k], counts[0, k]), matrices[0, k]), counts[0, k], 1
        )
        high = product.astype(jnp.bfloat16)
        left[2 * (k - 2)] = high
        left[2 * (k - 2) + 1] = (product - high.astype(jnp.float32)).astype(jnp.bfloat16)
    out[:, 0] = shares(contract_rows(own_basis[0], own_image[0]))
    image = times(matrices[0, 0], masked(x_above[...], counts[0, 0])).astype(jnp.bfloat16)
    along_x = contract_rows(masked(margin[0, 0], counts[0, 0]), image)
    out[:, 1] = shares(along_x)
    out[:, 2] = shares(along_x.T)


def far_kernel(left, near, *refs):
    out, received = refs[-1], list(refs[:-1])
    out[:, :3] = near[...]
    for k in range(2, 6):
        parts = [received.pop(0) for e in EXCHANGES.values() if e[1] == k]
        value = total(parts)
        block = times(left[2 * (k - 2)], value)
        if k % 2 == 0:
            block = block + times(left[2 * (k - 2) + 1], value)
        out[:, 1 + k] = shares(block)


def spread_kernel(rows, out):
    out[:, :2] = rows[:, :2].astype(jnp.float32)
    out[0, 2] = jnp.zeros((SHARE, EIG), jnp.float32)
    out[1:, 2] = rows[:-1, 2].astype(jnp.float32)
    out[:, 3:] = rows[:, 3:].astype(jnp.float32)


def on_chip(value):
    return pltpu.with_memory_space_constraint(value, pltpu.VMEM)


def local(margin_basis, pair_matrix, own_basis, own_image, tile_counts):
    smem = pl.BlockSpec(memory_space=pltpu.SMEM)
    vmem = pl.BlockSpec(memory_space=pltpu.VMEM)
    received = {}
    for name, (sent, serves, axis, steps, sends) in EXCHANGES.items():
        received[name] = on_chip(moved(margin_basis[0, sent], axis, steps, sends))
    near, left = pl.pallas_call(
        near_kernel,
        out_shape=(
            pltpu.VMEM((8, 3, SHARE, EIG), jnp.bfloat16),
            pltpu.VMEM((8, EIG, ROWS), jnp.bfloat16),
        ),
        in_specs=[smem] + [vmem] * 5,
        out_specs=(vmem, vmem),
    )(tile_counts, margin_basis, pair_matrix, own_basis, own_image, received["x_up"])
    arrived = [
        received[n] for k in range(2, 6) for n in ORDER if EXCHANGES[n][1] == k
    ]
    coarse = pl.pallas_call(
        far_kernel,
        out_shape=pltpu.VMEM((8, 7, SHARE, EIG), jnp.bfloat16),
        in_specs=[vmem] * (2 + len(arrived)),
        out_specs=vmem,
    )(on_chip(left), on_chip(near), *arrived)
    rows = lax.all_to_all(coarse, "grp", split_axis=0, concat_axis=0, tiled=True)
    return pl.pallas_call(
        spread_kernel,
        out_shape=jax.ShapeDtypeStruct((8, 7, SHARE, EIG), jnp.float32),
        in_specs=[vmem],
        out_specs=vmem,
    )(on_chip(rows))


def solution(mesh):
    return jax.shard_map(
        local,
        mesh=mesh,
        in_specs=(
            P(("sub", "grp"), None, None, None),
            P(("sub", "grp"), None, None, None),
            P(("sub", "grp"), None, None),
            P(("sub", "grp"), None, None),
            P(("sub", "grp"), None),
        ),
        out_specs=P("sub", None, "grp", None),
        check_vma=False,
    )
```

time: 61.6 us -> 58.8 us (0.955)
  the two profiles are of different devices: /device:TPU:56 before, /device:TPU:8 now
where the time goes in v2:
time: 58.8 us; the launch traced here: 58.5 us
  starting transfers between devices  29.1 us (49%)
  waiting for transfers between devices  13 us (22%)
  blocking collectives  11.3 us (19%)
  Pallas kernels  3.98 us (7%)
  local copies, waits for them, and re-layouts  1.11 us (2%)
    ppermute x5, starting transfers between devices, moved(): return lax.ppermute(value, axis, pairs)  29.1 us
    ppermute x5, waiting for transfers between devices, moved(): return lax.ppermute(value, axis, pairs)  13 us
    all_to_all x1, blocking collectives, local(): lax.all_to_all(coarse, 'grp', split_axis=0, concat_axis=0, tiled=True)  11.3 us
    pallas_call x1, Pallas kernels, local(): pl.pallas_call(near_kernel, out_shape=(pltpu.VMEM((8, 3, SHARE, EIG), jnp...  2.88 us
  transfers between devices with their start and end apart: 5, of which 1 were waited for; matrix products, arithmetic and copies ran while one was open for 0% of the time, Pallas kernels for 5%

profile of v2, /device:TPU:8, one launch (start us, length us, event | category | flops | bytes accessed | tf_op | source)
XLA Modules:
  0.0 58.5 jit_solution(6854938744092585556)
XLA Ops:
  0.0 1.1 %slice_bitcast_fusion = (bf16[384,128]{1,0:T(8,128)(2,1)S(1)}, bf16[384,128]{1,0:T(8,128)(2,1)S(1)}, bf16[384,128]{1,0:T(8,128)(2,1)S(1)}, bf16[384,128]{1,0:T(8,128)(2,1)S(1)}, bf16[384,128]{1,0:T(8,128)(2,1)S(1)}) fusion(bf16[1,6,384,128]{3,2,1,0:T(8,128)(2,1)} %margin.1), kind=kLoop, calls=%fused_computation | loop fusion | bytes 983040 | tf_op jit(solution)/shard_map/squeeze | solution.py:105
  1.1 1.3 %collective-permute-start = (bf16[384,128]{1,0:T(8,128)(2,1)S(1)}, bf16[384,128]{1,0:T(8,128)(2,1)S(1)}, u32[]{:S(2)}, u32[]{:S(2)}) collective-permute-start(bf16[384,128]{1,0:T(8,128)(2,1)S(1)} %get-tuple-element.12), channel_id=1, source_target_pairs={{1,0},{2,1},{3,2},{4,3},{5,4},{6,5},{7,6},{9,8},{10,9},{11,10},{12... | collective-permute-start | bytes 294920 | tf_op jit(solution)/shard_map/ppermute | solution.py:19
  2.4 15.7 %collective-permute-start.4 = (bf16[384,128]{1,0:T(8,128)(2,1)S(1)}, bf16[384,128]{1,0:T(8,128)(2,1)S(1)}, u32[]{:S(2)}, u32[]{:S(2)}) collective-permute-start(bf16[384,128]{1,0:T(8,128)(2,1)S(1)} %get-tuple-element.9), channel_id=1, source_target_pairs={{0,64},{8,72},{16,80},{24,88},{32,96},{40,104},{48,112},{56,120},{... | collective-permute-start | bytes 294920 | tf_op jit(solution)/shard_map/ppermute | solution.py:19
  18.2 2.9 %collective-permute-start.2 = (bf16[384,128]{1,0:T(8,128)(2,1)S(1)}, bf16[384,128]{1,0:T(8,128)(2,1)S(1)}, u32[]{:S(2)}, u32[]{:S(2)}) collective-permute-start(bf16[384,128]{1,0:T(8,128)(2,1)S(1)} %get-tuple-element.10), channel_id=1, source_target_pairs={{0,8},{8,16},{16,24},{24,32},{32,40},{40,48},{48,56},{56,64},{64,7... | collective-permute-start | bytes 294920 | tf_op jit(solution)/shard_map/ppermute | solution.py:19
  21.1 5.0 %collective-permute-start.1 = (bf16[384,128]{1,0:T(8,128)(2,1)S(1)}, bf16[384,128]{1,0:T(8,128)(2,1)S(1)}, u32[]{:S(2)}, u32[]{:S(2)}) collective-permute-start(bf16[384,128]{1,0:T(8,128)(2,1)S(1)} %get-tuple-element.11), channel_id=1, source_target_pairs={{8,0},{16,8},{24,16},{32,24},{40,32},{48,40},{56,48},{64,56},{72,6... | collective-permute-start | bytes 294920 | tf_op jit(solution)/shard_map/ppermute | solution.py:19
  26.1 4.1 %collective-permute-start.3 = (bf16[384,128]{1,0:T(8,128)(2,1)S(1)}, bf16[384,128]{1,0:T(8,128)(2,1)S(1)}, u32[]{:S(2)}, u32[]{:S(2)}) collective-permute-start(bf16[384,128]{1,0:T(8,128)(2,1)S(1)} %get-tuple-element.13), channel_id=1, source_target_pairs={{64,0},{72,8},{80,16},{88,24},{96,32},{104,40},{112,48},{120,56},{... | collective-permute-start | bytes 294920 | tf_op jit(solution)/shard_map/ppermute | solution.py:19
  30.2 0.0 collective-permute-done.x_above
  30.2 2.9 %shard_map.55 = (bf16[8,3,16,128]{3,2,1,0:T(8,128)(2,1)S(1)}, bf16[8,128,384]{2,1,0:T(8,128)(2,1)S(1)}) custom-call(s32[1,6]{1,0:T(1,128)} %counts.1, bf16[1,6,384,128]{3,2,1,0:T(8,128)(2,1)} %margin.1, bf16[1,6,384,384]{3,2,1,0:T(8,128)(2,1)} %matrices.1, bf16[1,2048,128]{2,1,0:T(8,128)(2,1)} %own_basis.1, bf16[1,2048,128]{2,1,0:T(8,128)(2,1)} %own_image.1, ...), custom_call_target="tpu_custom_call" | custom-call | tf_op jit(solution)/shard_map/pallas_call | solution.py:106
  33.1 0.0 collective-permute-done.4.refs_3_
  33.1 0.0 collective-permute-done.2.refs_1_
  33.1 0.0 collective-permute-done.1.refs_0_
  33.2 12.9 %collective-permute-done.3.refs_2_ = bf16[384,128]{1,0:T(8,128)(2,1)S(1)} collective-permute-done((bf16[384,128]{1,0:T(8,128)(2,1)S(1)}, bf16[384,128]{1,0:T(8,128)(2,1)S(1)}, u32[]{:S(2)}, u32[]{:S(2)}) %collective-permute-start.3) | collective-permute-done | bytes 98336 | tf_op jit(solution)/shard_map/ppermute | solution.py:19
  46.1 0.3 shard_map.56
  46.4 11.3 %all_to_all.5.rows = bf16[8,7,16,128]{3,2,1,0:T(8,128)(2,1)S(1)} all-to-all(bf16[8,7,16,128]{3,2,1,0:T(8,128)(2,1)S(1)} %shard_map.56), channel_id=1, replica_groups=mesh['sub'=64,'grp'=8] {'grp'}, dimensions={0} | all-to-all | bytes 458752 | tf_op jit(solution)/shard_map/all_to_all | solution.py:124
  57.7 0.8 %shard_map.57 = f32[8,7,16,128]{3,2,1,0:T(8,128)} custom-call(bf16[8,7,16,128]{3,2,1,0:T(8,128)(2,1)S(1)} %all_to_all.5.rows), custom_call_target="tpu_custom_call" | custom-call | tf_op jit(solution)/shard_map/pallas_call | solution.py:125
Async XLA Ops:
  1.1 29.1 %collective-permute-start = (bf16[384,128]{1,0:T(8,128)(2,1)S(1)}, bf16[384,128]{1,0:T(8,128)(2,1)S(1)}, u32[]{:S(2)}, u32[]{:S(2)}) collective-permute-start(bf16[384,128]{1,0:T(8,128)(2,1)S(1)} %get-tuple-element.12), channel_id=1, source_target_pairs={{1,0},{2,1},{3,2},{4,3},{5,4},{6,5},{7,6},{9,8},{10,9},{11,10},{12... | collective-permute-start | bytes 294920 | tf_op jit(solution)/shard_map/ppermute | solution.py:19
  2.4 30.7 %collective-permute-start.4 = (bf16[384,128]{1,0:T(8,128)(2,1)S(1)}, bf16[384,128]{1,0:T(8,128)(2,1)S(1)}, u32[]{:S(2)}, u32[]{:S(2)}) collective-permute-start(bf16[384,128]{1,0:T(8,128)(2,1)S(1)} %get-tuple-element.9), channel_id=1, source_target_pairs={{0,64},{8,72},{16,80},{24,88},{32,96},{40,104},{48,112},{56,120},{... | collective-permute-start | bytes 294920 | tf_op jit(solution)/shard_map/ppermute | solution.py:19
  18.2 15.0 %collective-permute-start.2 = (bf16[384,128]{1,0:T(8,128)(2,1)S(1)}, bf16[384,128]{1,0:T(8,128)(2,1)S(1)}, u32[]{:S(2)}, u32[]{:S(2)}) collective-permute-start(bf16[384,128]{1,0:T(8,128)(2,1)S(1)} %get-tuple-element.10), channel_id=1, source_target_pairs={{0,8},{8,16},{16,24},{24,32},{32,40},{40,48},{48,56},{56,64},{64,7... | collective-permute-start | bytes 294920 | tf_op jit(solution)/shard_map/ppermute | solution.py:19
  21.1 12.1 %collective-permute-start.1 = (bf16[384,128]{1,0:T(8,128)(2,1)S(1)}, bf16[384,128]{1,0:T(8,128)(2,1)S(1)}, u32[]{:S(2)}, u32[]{:S(2)}) collective-permute-start(bf16[384,128]{1,0:T(8,128)(2,1)S(1)} %get-tuple-element.11), channel_id=1, source_target_pairs={{8,0},{16,8},{24,16},{32,24},{40,32},{48,40},{56,48},{64,56},{72,6... | collective-permute-start | bytes 294920 | tf_op jit(solution)/shard_map/ppermute | solution.py:19
  26.1 20.0 %collective-permute-start.3 = (bf16[384,128]{1,0:T(8,128)(2,1)S(1)}, bf16[384,128]{1,0:T(8,128)(2,1)S(1)}, u32[]{:S(2)}, u32[]{:S(2)}) collective-permute-start(bf16[384,128]{1,0:T(8,128)(2,1)S(1)} %get-tuple-element.13), channel_id=1, source_target_pairs={{64,0},{72,8},{80,16},{88,24},{96,32},{104,40},{112,48},{120,56},{... | collective-permute-start | bytes 294920 | tf_op jit(solution)/shard_map/ppermute | solution.py:19

commit v3 on v2

--- a/solution.py
+++ b/solution.py
@@ -23,14 +23,32 @@
     return True
 
 
+def far_side(line):
+    return line % (2 * SPAN) >= SPAN
+
+
+def near_side(line):
+    return line % (2 * SPAN) < SPAN
+
+
+def steps_to_start(line):
+    return line % (2 * SPAN) == 1
+
+
+def not_to_start(line):
+    return not steps_to_start(line)
+
+
 EXCHANGES = {
-    "z_up": (5, 4, "sub", -SPAN, anyone),
+    "z_up_first": (5, 4, "sub", -SPAN, far_side),
+    "y_up_start": (3, 2, "sub", -1, steps_to_start),
     "z_down": (4, 5, "sub", SPAN, anyone),
+    "z_up_last": (5, 4, "sub", -SPAN, near_side),
+    "y_down": (2, 3, "sub", 1, anyone),
     "x_up": (1, 0, "grp", -1, anyone),
-    "y_up": (3, 2, "sub", -1, anyone),
-    "y_down": (2, 3, "sub", 1, anyone),
+    "y_up": (3, 2, "sub", -1, not_to_start),
 }
-ORDER = tuple(EXCHANGES)
+SLOTS = (0, 2, 3, 4, 5)
 
 
 def masked(block, tile_count, dim=0):
@@ -59,31 +77,30 @@
     return value
 
 
-def near_kernel(counts, margin, matrices, own_basis, own_image, x_above, out, left):
-    for k in range(2, 6):
+def near_kernel(counts, margin, matrices, own_basis, own_image, out, left):
+    for place, k in enumerate(SLOTS):
         product = masked(
             contract_rows(masked(margin[0, k], counts[0, k]), matrices[0, k]), counts[0, k], 1
         )
         high = product.astype(jnp.bfloat16)
-        left[2 * (k - 2)] = high
-        left[2 * (k - 2) + 1] = (product - high.astype(jnp.float32)).astype(jnp.bfloat16)
-    out[:, 0] = shares(contract_rows(own_basis[0], own_image[0]))
-    image = times(matrices[0, 0], masked(x_above[...], counts[0, 0])).astype(jnp.bfloat16)
-    along_x = contract_rows(masked(margin[0, 0], counts[0, 0]), image)
-    out[:, 1] = shares(along_x)
-    out[:, 2] = shares(along_x.T)
+        left[2 * place] = high
+        if k % 2 == 0:
+            left[2 * place + 1] = (product - high.astype(jnp.float32)).astype(jnp.bfloat16)
+    out[...] = shares(contract_rows(own_basis[0], own_image[0]))
 
 
 def far_kernel(left, near, *refs):
     out, received = refs[-1], list(refs[:-1])
-    out[:, :3] = near[...]
-    for k in range(2, 6):
+    out[:, 0] = near[...]
+    for place, k in enumerate(SLOTS):
         parts = [received.pop(0) for e in EXCHANGES.values() if e[1] == k]
         value = total(parts)
-        block = times(left[2 * (k - 2)], value)
+        block = times(left[2 * place], value)
         if k % 2 == 0:
-            block = block + times(left[2 * (k - 2) + 1], value)
+            block = block + times(left[2 * place + 1], value)
         out[:, 1 + k] = shares(block)
+        if k == 0:
+            out[:, 2] = shares(block.T)
 
 
 def spread_kernel(rows, out):
@@ -106,14 +123,14 @@
     near, left = pl.pallas_call(
         near_kernel,
         out_shape=(
-            pltpu.VMEM((8, 3, SHARE, EIG), jnp.bfloat16),
-            pltpu.VMEM((8, EIG, ROWS), jnp.bfloat16),
+            pltpu.VMEM((8, SHARE, EIG), jnp.bfloat16),
+            pltpu.VMEM((2 * len(SLOTS), EIG, ROWS), jnp.bfloat16),
         ),
-        in_specs=[smem] + [vmem] * 5,
+        in_specs=[smem] + [vmem] * 4,
         out_specs=(vmem, vmem),
-    )(tile_counts, margin_basis, pair_matrix, own_basis, own_image, received["x_up"])
+    )(tile_counts, margin_basis, pair_matrix, own_basis, own_image)
     arrived = [
-        received[n] for k in range(2, 6) for n in ORDER if EXCHANGES[n][1] == k
+        received[n] for k in SLOTS for n in EXCHANGES if EXCHANGES[n][1] == k
     ]
     coarse = pl.pallas_call(
         far_kernel,

time: 58.8 us -> 67.7 us (1.15)
  the two profiles are of different devices: /device:TPU:8 before, /device:TPU:40 now
where the time goes in v3:
time: 67.7 us; the launch traced here: 67.4 us
  starting transfers between devices  37.7 us (56%)
  waiting for transfers between devices  13.4 us (20%)
  blocking collectives  11.3 us (17%)
  Pallas kernels  3.76 us (6%)
  local copies, waits for them, and re-layouts  1.11 us (2%)
    ppermute x7, starting transfers between devices, moved(): return lax.ppermute(value, axis, pairs)  37.7 us
    ppermute x7, waiting for transfers between devices, moved(): return lax.ppermute(value, axis, pairs)  13.4 us
    all_to_all x1, blocking collectives, local(): lax.all_to_all(coarse, 'grp', split_axis=0, concat_axis=0, tiled=True)  11.3 us
    pallas_call x1, Pallas kernels, local(): pl.pallas_call(near_kernel, out_shape=(pltpu.VMEM((8, SHARE, EIG), jnp.bf...  2.6 us
  transfers between devices with their start and end apart: 7, of which 1 were waited for; matrix products, arithmetic and copies ran while one was open for 0% of the time, Pallas kernels for 4%

profile of v3, /device:TPU:40, one launch (start us, length us, event | category | flops | bytes accessed | tf_op | source)
XLA Modules:
  0.0 67.4 jit_solution(16295791508566408943)
XLA Ops:
  0.0 1.1 %slice_bitcast_fusion = (bf16[384,128]{1,0:T(8,128)(2,1)S(1)}, bf16[384,128]{1,0:T(8,128)(2,1)S(1)}, bf16[384,128]{1,0:T(8,128)(2,1)S(1)}, bf16[384,128]{1,0:T(8,128)(2,1)S(1)}, bf16[384,128]{1,0:T(8,128)(2,1)S(1)}) fusion(bf16[1,6,384,128]{3,2,1,0:T(8,128)(2,1)} %margin.1), kind=kLoop, calls=%fused_computation | loop fusion | bytes 983040 | tf_op jit(solution)/shard_map/squeeze | solution.py:122
  1.1 14.8 %collective-permute-start.6 = (bf16[384,128]{1,0:T(8,128)(2,1)S(1)}, bf16[384,128]{1,0:T(8,128)(2,1)S(1)}, u32[]{:S(2)}, u32[]{:S(2)}) collective-permute-start(bf16[384,128]{1,0:T(8,128)(2,1)S(1)} %get-tuple-element.9), channel_id=1, source_target_pairs={{0,64},{8,72},{16,80},{24,88},{32,96},{40,104},{48,112},{56,120},{... | collective-permute-start | bytes 294920 | tf_op jit(solution)/shard_map/ppermute | solution.py:19
  16.0 2.9 %collective-permute-start.3 = (bf16[384,128]{1,0:T(8,128)(2,1)S(1)}, bf16[384,128]{1,0:T(8,128)(2,1)S(1)}, u32[]{:S(2)}, u32[]{:S(2)}) collective-permute-start(bf16[384,128]{1,0:T(8,128)(2,1)S(1)} %get-tuple-element.10), channel_id=1, source_target_pairs={{0,8},{8,16},{16,24},{24,32},{32,40},{40,48},{48,56},{56,64},{64,7... | collective-permute-start | bytes 294920 | tf_op jit(solution)/shard_map/ppermute | solution.py:19
  18.9 1.3 %collective-permute-start.2 = (bf16[384,128]{1,0:T(8,128)(2,1)S(1)}, bf16[384,128]{1,0:T(8,128)(2,1)S(1)}, u32[]{:S(2)}, u32[]{:S(2)}) collective-permute-start(bf16[384,128]{1,0:T(8,128)(2,1)S(1)} %get-tuple-element.11), channel_id=1, source_target_pairs={{16,8},{24,16},{32,24},{40,32},{48,40},{56,48},{64,56},{72,64},{80... | collective-permute-start | bytes 294920 | tf_op jit(solution)/shard_map/ppermute | solution.py:19
  20.2 6.7 %collective-permute-start.1 = (bf16[384,128]{1,0:T(8,128)(2,1)S(1)}, bf16[384,128]{1,0:T(8,128)(2,1)S(1)}, u32[]{:S(2)}, u32[]{:S(2)}) collective-permute-start(bf16[384,128]{1,0:T(8,128)(2,1)S(1)} %get-tuple-element.11), channel_id=1, source_target_pairs={{8,0},{136,128},{264,256},{392,384},{9,1},{137,129},{265,257},{393... | collective-permute-start | bytes 294920 | tf_op jit(solution)/shard_map/ppermute | solution.py:19
  26.8 1.3 %collective-permute-start = (bf16[384,128]{1,0:T(8,128)(2,1)S(1)}, bf16[384,128]{1,0:T(8,128)(2,1)S(1)}, u32[]{:S(2)}, u32[]{:S(2)}) collective-permute-start(bf16[384,128]{1,0:T(8,128)(2,1)S(1)} %get-tuple-element.12), channel_id=1, source_target_pairs={{1,0},{2,1},{3,2},{4,3},{5,4},{6,5},{7,6},{9,8},{10,9},{11,10},{12... | collective-permute-start | bytes 294920 | tf_op jit(solution)/shard_map/ppermute | solution.py:19
  28.1 0.0 collective-permute-done.6.refs_6_
  28.2 9.4 %collective-permute-start.5 = (bf16[384,128]{1,0:T(8,128)(2,1)S(1)}, bf16[384,128]{1,0:T(8,128)(2,1)S(1)}, u32[]{:S(2)}, u32[]{:S(2)}) collective-permute-start(bf16[384,128]{1,0:T(8,128)(2,1)S(1)} %get-tuple-element.13), channel_id=1, source_target_pairs={{128,64},{136,72},{144,80},{152,88},{160,96},{168,104},{176,112},{... | collective-permute-start | bytes 294920 | tf_op jit(solution)/shard_map/ppermute | solution.py:19
  37.6 0.0 collective-permute-done.3.refs_3_
  37.6 1.3 %collective-permute-start.4 = (bf16[384,128]{1,0:T(8,128)(2,1)S(1)}, bf16[384,128]{1,0:T(8,128)(2,1)S(1)}, u32[]{:S(2)}, u32[]{:S(2)}) collective-permute-start(bf16[384,128]{1,0:T(8,128)(2,1)S(1)} %get-tuple-element.13), channel_id=1, source_target_pairs={{64,0},{72,8},{80,16},{88,24},{96,32},{104,40},{112,48},{120,56},{... | collective-permute-start | bytes 294920 | tf_op jit(solution)/shard_map/ppermute | solution.py:19
  38.9 2.6 %shard_map.55 = (bf16[8,16,128]{2,1,0:T(8,128)(2,1)S(1)}, bf16[10,128,384]{2,1,0:T(8,128)(2,1)S(1)}) custom-call(s32[1,6]{1,0:T(1,128)} %counts.1, bf16[1,6,384,128]{3,2,1,0:T(8,128)(2,1)} %margin.1, bf16[1,6,384,384]{3,2,1,0:T(8,128)(2,1)} %matrices.1, bf16[1,2048,128]{2,1,0:T(8,128)(2,1)} %own_basis.1, bf16[1,2048,128]{2,1,0:T(8,128)(2,1)} %own_image.1), custom_call_target="tpu_custom_call" | custom-call | tf_op jit(solution)/shard_map/pallas_call | solution.py:123
  41.5 0.0 collective-permute-done.refs_0_
  41.5 0.0 collective-permute-done.2.refs_2_
  41.5 0.0 collective-permute-done.1.refs_1_
  41.5 0.0 collective-permute-done.5.refs_5_
  41.5 13.4 %collective-permute-done.4.refs_4_ = bf16[384,128]{1,0:T(8,128)(2,1)S(1)} collective-permute-done((bf16[384,128]{1,0:T(8,128)(2,1)S(1)}, bf16[384,128]{1,0:T(8,128)(2,1)S(1)}, u32[]{:S(2)}, u32[]{:S(2)}) %collective-permute-start.4) | collective-permute-done | bytes 98336 | tf_op jit(solution)/shard_map/ppermute | solution.py:19
  54.9 0.4 shard_map.56
  55.3 11.3 %all_to_all.5.rows = bf16[8,7,16,128]{3,2,1,0:T(8,128)(2,1)S(1)} all-to-all(bf16[8,7,16,128]{3,2,1,0:T(8,128)(2,1)S(1)} %shard_map.56), channel_id=1, replica_groups=mesh['sub'=64,'grp'=8] {'grp'}, dimensions={0} | all-to-all | bytes 458752 | tf_op jit(solution)/shard_map/all_to_all | solution.py:141
  66.6 0.8 %shard_map.57 = f32[8,7,16,128]{3,2,1,0:T(8,128)} custom-call(bf16[8,7,16,128]{3,2,1,0:T(8,128)(2,1)S(1)} %all_to_all.5.rows), custom_call_target="tpu_custom_call" | custom-call | tf_op jit(solution)/shard_map/pallas_call | solution.py:142
Async XLA Ops:
  1.1 27.0 %collective-permute-start.6 = (bf16[384,128]{1,0:T(8,128)(2,1)S(1)}, bf16[384,128]{1,0:T(8,128)(2,1)S(1)}, u32[]{:S(2)}, u32[]{:S(2)}) collective-permute-start(bf16[384,128]{1,0:T(8,128)(2,1)S(1)} %get-tuple-element.9), channel_id=1, source_target_pairs={{0,64},{8,72},{16,80},{24,88},{32,96},{40,104},{48,112},{56,120},{... | collective-permute-start | bytes 294920 | tf_op jit(solution)/shard_map/ppermute | solution.py:19
  16.0 21.6 %collective-permute-start.3 = (bf16[384,128]{1,0:T(8,128)(2,1)S(1)}, bf16[384,128]{1,0:T(8,128)(2,1)S(1)}, u32[]{:S(2)}, u32[]{:S(2)}) collective-permute-start(bf16[384,128]{1,0:T(8,128)(2,1)S(1)} %get-tuple-element.10), channel_id=1, source_target_pairs={{0,8},{8,16},{16,24},{24,32},{32,40},{40,48},{48,56},{56,64},{64,7... | collective-permute-start | bytes 294920 | tf_op jit(solution)/shard_map/ppermute | solution.py:19
  18.9 22.6 %collective-permute-start.2 = (bf16[384,128]{1,0:T(8,128)(2,1)S(1)}, bf16[384,128]{1,0:T(8,128)(2,1)S(1)}, u32[]{:S(2)}, u32[]{:S(2)}) collective-permute-start(bf16[384,128]{1,0:T(8,128)(2,1)S(1)} %get-tuple-element.11), channel_id=1, source_target_pairs={{16,8},{24,16},{32,24},{40,32},{48,40},{56,48},{64,56},{72,64},{80... | collective-permute-start | bytes 294920 | tf_op jit(solution)/shard_map/ppermute | solution.py:19
  20.2 21.3 %collective-permute-start.1 = (bf16[384,128]{1,0:T(8,128)(2,1)S(1)}, bf16[384,128]{1,0:T(8,128)(2,1)S(1)}, u32[]{:S(2)}, u32[]{:S(2)}) collective-permute-start(bf16[384,128]{1,0:T(8,128)(2,1)S(1)} %get-tuple-element.11), channel_id=1, source_target_pairs={{8,0},{136,128},{264,256},{392,384},{9,1},{137,129},{265,257},{393... | collective-permute-start | bytes 294920 | tf_op jit(solution)/shard_map/ppermute | solution.py:19
  26.8 14.6 %collective-permute-start = (bf16[384,128]{1,0:T(8,128)(2,1)S(1)}, bf16[384,128]{1,0:T(8,128)(2,1)S(1)}, u32[]{:S(2)}, u32[]{:S(2)}) collective-permute-start(bf16[384,128]{1,0:T(8,128)(2,1)S(1)} %get-tuple-element.12), channel_id=1, source_target_pairs={{1,0},{2,1},{3,2},{4,3},{5,4},{6,5},{7,6},{9,8},{10,9},{11,10},{12... | collective-permute-start | bytes 294920 | tf_op jit(solution)/shard_map/ppermute | solution.py:19
  28.2 13.4 %collective-permute-start.5 = (bf16[384,128]{1,0:T(8,128)(2,1)S(1)}, bf16[384,128]{1,0:T(8,128)(2,1)S(1)}, u32[]{:S(2)}, u32[]{:S(2)}) collective-permute-start(bf16[384,128]{1,0:T(8,128)(2,1)S(1)} %get-tuple-element.13), channel_id=1, source_target_pairs={{128,64},{136,72},{144,80},{152,88},{160,96},{168,104},{176,112},{... | collective-permute-start | bytes 294920 | tf_op jit(solution)/shard_map/ppermute | solution.py:19
  37.6 17.4 %collective-permute-start.4 = (bf16[384,128]{1,0:T(8,128)(2,1)S(1)}, bf16[384,128]{1,0:T(8,128)(2,1)S(1)}, u32[]{:S(2)}, u32[]{:S(2)}) collective-permute-start(bf16[384,128]{1,0:T(8,128)(2,1)S(1)} %get-tuple-element.13), channel_id=1, source_target_pairs={{64,0},{72,8},{80,16},{88,24},{96,32},{104,40},{112,48},{120,56},{... | collective-permute-start | bytes 294920 | tf_op jit(solution)/shard_map/ppermute | solution.py:19

commit v4 on v3

--- a/solution.py
+++ b/solution.py
@@ -31,22 +31,27 @@
     return line % (2 * SPAN) < SPAN
 
 
+def turns_down(line):
+    return line % (2 * SPAN) == 0
+
+
 def steps_to_start(line):
     return line % (2 * SPAN) == 1
 
 
-def not_to_start(line):
-    return not steps_to_start(line)
+def inner_rest(line):
+    return line % (2 * SPAN) > 1
 
 
 EXCHANGES = {
     "z_up_first": (5, 4, "sub", -SPAN, far_side),
     "y_up_start": (3, 2, "sub", -1, steps_to_start),
     "z_down": (4, 5, "sub", SPAN, anyone),
+    "y_up_turn": (3, 2, "sub", -1, turns_down),
     "z_up_last": (5, 4, "sub", -SPAN, near_side),
+    "x_up": (1, 0, "grp", -1, anyone),
     "y_down": (2, 3, "sub", 1, anyone),
-    "x_up": (1, 0, "grp", -1, anyone),
-    "y_up": (3, 2, "sub", -1, not_to_start),
+    "y_up": (3, 2, "sub", -1, inner_rest),
 }
 SLOTS = (0, 2, 3, 4, 5)
 

time: 67.7 us -> 62.1 us (0.917)
  the two profiles are of different devices: /device:TPU:40 before, /device:TPU:24 now
where the time goes in v4:
time: 62.1 us; the launch traced here: 61.8 us
  starting transfers between devices  40.1 us (65%)
  blocking collectives  11.5 us (19%)
  waiting for transfers between devices  5.14 us (8%)
  Pallas kernels  3.76 us (6%)
  local copies, waits for them, and re-layouts  1.11 us (2%)
    ppermute x8, starting transfers between devices, moved(): return lax.ppermute(value, axis, pairs)  40.1 us
    all_to_all x1, blocking collectives, local(): lax.all_to_all(coarse, 'grp', split_axis=0, concat_axis=0, tiled=True)  11.5 us
    ppermute x8, waiting for transfers between devices, moved(): return lax.ppermute(value, axis, pairs)  5.14 us
    pallas_call x1, Pallas kernels, local(): pl.pallas_call(near_kernel, out_shape=(pltpu.VMEM((8, SHARE, EIG), jnp.bf...  2.6 us
  transfers between devices with their start and end apart: 8, of which 2 were waited for; matrix products, arithmetic and copies ran while one was open for 0% of the time, Pallas kernels for 4%

profile of v4, /device:TPU:24, one launch (start us, length us, event | category | flops | bytes accessed | tf_op | source)
XLA Modules:
  0.0 61.8 jit_solution(15431837789757032210)
XLA Ops:
  0.0 1.1 %slice_bitcast_fusion = (bf16[384,128]{1,0:T(8,128)(2,1)S(1)}, bf16[384,128]{1,0:T(8,128)(2,1)S(1)}, bf16[384,128]{1,0:T(8,128)(2,1)S(1)}, bf16[384,128]{1,0:T(8,128)(2,1)S(1)}, bf16[384,128]{1,0:T(8,128)(2,1)S(1)}) fusion(bf16[1,6,384,128]{3,2,1,0:T(8,128)(2,1)} %margin.1), kind=kLoop, calls=%fused_computation | loop fusion | bytes 983040 | tf_op jit(solution)/shard_map/squeeze | solution.py:127
  1.1 15.7 %collective-permute-start.7 = (bf16[384,128]{1,0:T(8,128)(2,1)S(1)}, bf16[384,128]{1,0:T(8,128)(2,1)S(1)}, u32[]{:S(2)}, u32[]{:S(2)}) collective-permute-start(bf16[384,128]{1,0:T(8,128)(2,1)S(1)} %get-tuple-element.9), channel_id=1, source_target_pairs={{0,64},{8,72},{16,80},{24,88},{32,96},{40,104},{48,112},{56,120},{... | collective-permute-start | bytes 294920 | tf_op jit(solution)/shard_map/ppermute | solution.py:19
  16.9 2.9 %collective-permute-start.4 = (bf16[384,128]{1,0:T(8,128)(2,1)S(1)}, bf16[384,128]{1,0:T(8,128)(2,1)S(1)}, u32[]{:S(2)}, u32[]{:S(2)}) collective-permute-start(bf16[384,128]{1,0:T(8,128)(2,1)S(1)} %get-tuple-element.10), channel_id=1, source_target_pairs={{0,8},{8,16},{16,24},{24,32},{32,40},{40,48},{48,56},{56,64},{64,7... | collective-permute-start | bytes 294920 | tf_op jit(solution)/shard_map/ppermute | solution.py:19
  19.8 1.3 %collective-permute-start = (bf16[384,128]{1,0:T(8,128)(2,1)S(1)}, bf16[384,128]{1,0:T(8,128)(2,1)S(1)}, u32[]{:S(2)}, u32[]{:S(2)}) collective-permute-start(bf16[384,128]{1,0:T(8,128)(2,1)S(1)} %get-tuple-element.12), channel_id=1, source_target_pairs={{1,0},{2,1},{3,2},{4,3},{5,4},{6,5},{7,6},{9,8},{10,9},{11,10},{12... | collective-permute-start | bytes 294920 | tf_op jit(solution)/shard_map/ppermute | solution.py:19
  21.1 2.1 %collective-permute-start.6 = (bf16[384,128]{1,0:T(8,128)(2,1)S(1)}, bf16[384,128]{1,0:T(8,128)(2,1)S(1)}, u32[]{:S(2)}, u32[]{:S(2)}) collective-permute-start(bf16[384,128]{1,0:T(8,128)(2,1)S(1)} %get-tuple-element.13), channel_id=1, source_target_pairs={{128,64},{136,72},{144,80},{152,88},{160,96},{168,104},{176,112},{... | collective-permute-start | bytes 294920 | tf_op jit(solution)/shard_map/ppermute | solution.py:19
  23.2 1.3 %collective-permute-start.5 = (bf16[384,128]{1,0:T(8,128)(2,1)S(1)}, bf16[384,128]{1,0:T(8,128)(2,1)S(1)}, u32[]{:S(2)}, u32[]{:S(2)}) collective-permute-start(bf16[384,128]{1,0:T(8,128)(2,1)S(1)} %get-tuple-element.13), channel_id=1, source_target_pairs={{64,0},{72,8},{80,16},{88,24},{96,32},{104,40},{112,48},{120,56},{... | collective-permute-start | bytes 294920 | tf_op jit(solution)/shard_map/ppermute | solution.py:19
  24.5 0.0 collective-permute-done.7.refs_7_
  24.5 0.7 %collective-permute-start.3 = (bf16[384,128]{1,0:T(8,128)(2,1)S(1)}, bf16[384,128]{1,0:T(8,128)(2,1)S(1)}, u32[]{:S(2)}, u32[]{:S(2)}) collective-permute-start(bf16[384,128]{1,0:T(8,128)(2,1)S(1)} %get-tuple-element.11), channel_id=1, source_target_pairs={{16,8},{24,16},{32,24},{40,32},{48,40},{56,48},{64,56},{72,64},{80... | collective-permute-start | bytes 294920 | tf_op jit(solution)/shard_map/ppermute | solution.py:19
  25.2 2.2 %collective-permute-done.4.refs_4_ = bf16[384,128]{1,0:T(8,128)(2,1)S(1)} collective-permute-done((bf16[384,128]{1,0:T(8,128)(2,1)S(1)}, bf16[384,128]{1,0:T(8,128)(2,1)S(1)}, u32[]{:S(2)}, u32[]{:S(2)}) %collective-permute-start.4) | collective-permute-done | bytes 98336 | tf_op jit(solution)/shard_map/ppermute | solution.py:19
  27.4 14.8 %collective-permute-start.2 = (bf16[384,128]{1,0:T(8,128)(2,1)S(1)}, bf16[384,128]{1,0:T(8,128)(2,1)S(1)}, u32[]{:S(2)}, u32[]{:S(2)}) collective-permute-start(bf16[384,128]{1,0:T(8,128)(2,1)S(1)} %get-tuple-element.11), channel_id=1, source_target_pairs={{128,120},{256,248},{384,376},{129,121},{257,249},{385,377},{130,1... | collective-permute-start | bytes 294920 | tf_op jit(solution)/shard_map/ppermute | solution.py:19
  42.2 0.0 collective-permute-done.refs_0_
  42.2 1.3 %collective-permute-start.1 = (bf16[384,128]{1,0:T(8,128)(2,1)S(1)}, bf16[384,128]{1,0:T(8,128)(2,1)S(1)}, u32[]{:S(2)}, u32[]{:S(2)}) collective-permute-start(bf16[384,128]{1,0:T(8,128)(2,1)S(1)} %get-tuple-element.11), channel_id=1, source_target_pairs={{8,0},{136,128},{264,256},{392,384},{9,1},{137,129},{265,257},{393... | collective-permute-start | bytes 294920 | tf_op jit(solution)/shard_map/ppermute | solution.py:19
  43.5 2.6 %shard_map.55 = (bf16[8,16,128]{2,1,0:T(8,128)(2,1)S(1)}, bf16[10,128,384]{2,1,0:T(8,128)(2,1)S(1)}) custom-call(s32[1,6]{1,0:T(1,128)} %counts.1, bf16[1,6,384,128]{3,2,1,0:T(8,128)(2,1)} %margin.1, bf16[1,6,384,384]{3,2,1,0:T(8,128)(2,1)} %matrices.1, bf16[1,2048,128]{2,1,0:T(8,128)(2,1)} %own_basis.1, bf16[1,2048,128]{2,1,0:T(8,128)(2,1)} %own_image.1), custom_call_target="tpu_custom_call" | custom-call | tf_op jit(solution)/shard_map/pallas_call | solution.py:128
  46.1 0.0 collective-permute-done.6.refs_6_
  46.1 0.0 collective-permute-done.5.refs_5_
  46.1 0.0 collective-permute-done.3.refs_3_
  46.1 0.0 collective-permute-done.2.refs_2_
  46.2 2.9 %collective-permute-done.1.refs_1_ = bf16[384,128]{1,0:T(8,128)(2,1)S(1)} collective-permute-done((bf16[384,128]{1,0:T(8,128)(2,1)S(1)}, bf16[384,128]{1,0:T(8,128)(2,1)S(1)}, u32[]{:S(2)}, u32[]{:S(2)}) %collective-permute-start.1) | collective-permute-done | bytes 98336 | tf_op jit(solution)/shard_map/ppermute | solution.py:19
  49.1 0.4 shard_map.56
  49.5 11.5 %all_to_all.5.rows = bf16[8,7,16,128]{3,2,1,0:T(8,128)(2,1)S(1)} all-to-all(bf16[8,7,16,128]{3,2,1,0:T(8,128)(2,1)S(1)} %shard_map.56), channel_id=1, replica_groups=mesh['sub'=64,'grp'=8] {'grp'}, dimensions={0} | all-to-all | bytes 458752 | tf_op jit(solution)/shard_map/all_to_all | solution.py:146
  61.0 0.8 %shard_map.57 = f32[8,7,16,128]{3,2,1,0:T(8,128)} custom-call(bf16[8,7,16,128]{3,2,1,0:T(8,128)(2,1)S(1)} %all_to_all.5.rows), custom_call_target="tpu_custom_call" | custom-call | tf_op jit(solution)/shard_map/pallas_call | solution.py:147
Async XLA Ops:
  1.1 23.4 %collective-permute-start.7 = (bf16[384,128]{1,0:T(8,128)(2,1)S(1)}, bf16[384,128]{1,0:T(8,128)(2,1)S(1)}, u32[]{:S(2)}, u32[]{:S(2)}) collective-permute-start(bf16[384,128]{1,0:T(8,128)(2,1)S(1)} %get-tuple-element.9), channel_id=1, source_target_pairs={{0,64},{8,72},{16,80},{24,88},{32,96},{40,104},{48,112},{56,120},{... | collective-permute-start | bytes 294920 | tf_op jit(solution)/shard_map/ppermute | solution.py:19
  16.9 10.5 %collective-permute-start.4 = (bf16[384,128]{1,0:T(8,128)(2,1)S(1)}, bf16[384,128]{1,0:T(8,128)(2,1)S(1)}, u32[]{:S(2)}, u32[]{:S(2)}) collective-permute-start(bf16[384,128]{1,0:T(8,128)(2,1)S(1)} %get-tuple-element.10), channel_id=1, source_target_pairs={{0,8},{8,16},{16,24},{24,32},{32,40},{40,48},{48,56},{56,64},{64,7... | collective-permute-start | bytes 294920 | tf_op jit(solution)/shard_map/ppermute | solution.py:19
  19.8 22.4 %collective-permute-start = (bf16[384,128]{1,0:T(8,128)(2,1)S(1)}, bf16[384,128]{1,0:T(8,128)(2,1)S(1)}, u32[]{:S(2)}, u32[]{:S(2)}) collective-permute-start(bf16[384,128]{1,0:T(8,128)(2,1)S(1)} %get-tuple-element.12), channel_id=1, source_target_pairs={{1,0},{2,1},{3,2},{4,3},{5,4},{6,5},{7,6},{9,8},{10,9},{11,10},{12... | collective-permute-start | bytes 294920 | tf_op jit(solution)/shard_map/ppermute | solution.py:19
  21.1 25.0 %collective-permute-start.6 = (bf16[384,128]{1,0:T(8,128)(2,1)S(1)}, bf16[384,128]{1,0:T(8,128)(2,1)S(1)}, u32[]{:S(2)}, u32[]{:S(2)}) collective-permute-start(bf16[384,128]{1,0:T(8,128)(2,1)S(1)} %get-tuple-element.13), channel_id=1, source_target_pairs={{128,64},{136,72},{144,80},{152,88},{160,96},{168,104},{176,112},{... | collective-permute-start | bytes 294920 | tf_op jit(solution)/shard_map/ppermute | solution.py:19
  23.2 22.9 %collective-permute-start.5 = (bf16[384,128]{1,0:T(8,128)(2,1)S(1)}, bf16[384,128]{1,0:T(8,128)(2,1)S(1)}, u32[]{:S(2)}, u32[]{:S(2)}) collective-permute-start(bf16[384,128]{1,0:T(8,128)(2,1)S(1)} %get-tuple-element.13), channel_id=1, source_target_pairs={{64,0},{72,8},{80,16},{88,24},{96,32},{104,40},{112,48},{120,56},{... | collective-permute-start | bytes 294920 | tf_op jit(solution)/shard_map/ppermute | solution.py:19
  24.5 21.6 %collective-permute-start.3 = (bf16[384,128]{1,0:T(8,128)(2,1)S(1)}, bf16[384,128]{1,0:T(8,128)(2,1)S(1)}, u32[]{:S(2)}, u32[]{:S(2)}) collective-permute-start(bf16[384,128]{1,0:T(8,128)(2,1)S(1)} %get-tuple-element.11), channel_id=1, source_target_pairs={{16,8},{24,16},{32,24},{40,32},{48,40},{56,48},{64,56},{72,64},{80... | collective-permute-start | bytes 294920 | tf_op jit(solution)/shard_map/ppermute | solution.py:19
  27.4 18.8 %collective-permute-start.2 = (bf16[384,128]{1,0:T(8,128)(2,1)S(1)}, bf16[384,128]{1,0:T(8,128)(2,1)S(1)}, u32[]{:S(2)}, u32[]{:S(2)}) collective-permute-start(bf16[384,128]{1,0:T(8,128)(2,1)S(1)} %get-tuple-element.11), channel_id=1, source_target_pairs={{128,120},{256,248},{384,376},{129,121},{257,249},{385,377},{130,1... | collective-permute-start | bytes 294920 | tf_op jit(solution)/shard_map/ppermute | solution.py:19
  42.2 6.9 %collective-permute-start.1 = (bf16[384,128]{1,0:T(8,128)(2,1)S(1)}, bf16[384,128]{1,0:T(8,128)(2,1)S(1)}, u32[]{:S(2)}, u32[]{:S(2)}) collective-permute-start(bf16[384,128]{1,0:T(8,128)(2,1)S(1)} %get-tuple-element.11), channel_id=1, source_target_pairs={{8,0},{136,128},{264,256},{392,384},{9,1},{137,129},{265,257},{393... | collective-permute-start | bytes 294920 | tf_op jit(solution)/shard_map/ppermute | solution.py:19
